TPU v7x, 32 devices: a whole 2x2x4 slice. The times are simulated.
32 devices in a mesh: rows: 16 (over z, y, core), heads: 2 (over x).
Axes of the slice: x: 2, y: 2, z: 4, core: 2. Of those that a mesh axis runs over, the one named last changes fastest.
Arguments:
- features: bfloat16 [8192, 1664], P(('rows', 'heads')), may hold values from -6 to 6
- segment_ids: int32 [8192], P(('rows', 'heads')), may hold values from 0 to 1, as said below
- padding_mask: int32 [8192], P(('rows', 'heads')), may hold values from 0 to 1, as said below
- w_proj: bfloat16 [1664, 1024], replicated, may hold values from -0.15625 to 0.15625
- proj_bias: float32 [1024], replicated, may hold values from -3 to 3
- gain_attn: float32 [1024], replicated, may hold values from 0.1 to 1.9
- w_qkv: bfloat16 [1024, 3, 1024], P(None, None, 'heads'), may hold values from -0.09375 to 0.09375
- w_out: bfloat16 [1024, 1024], P('heads'), may hold values from -3 to 3
- gain_ffn: float32 [1024], replicated, may hold values from 0.1 to 1.9
- w_gate_up: bfloat16 [1024, 2, 2816], P(None, None, 'heads'), may hold values from -0.1875 to 0.1875
- w_down: bfloat16 [2816, 1024], P('heads'), may hold values from -0.109375 to 0.109375
- cotangent: bfloat16 [8192, 1024], P(('rows', 'heads')), may hold values from -6 to 6
Outputs:
- layer_out: bfloat16 [8192, 1024], P(('rows', 'heads'))
- grad_features: float32 [8192, 1664], P(('rows', 'heads'))
- grad_proj: float32 [1664, 1024], replicated
- grad_bias: float32 [1024], replicated
- grad_gain_attn: float32 [1024], replicated
- grad_qkv: float32 [1024, 3, 1024], P(None, None, 'heads')
- grad_out: float32 [1024, 1024], P('heads')
- grad_gain_ffn: float32 [1024], replicated
- grad_gate_up: float32 [1024, 2, 2816], P(None, None, 'heads')
- grad_down: float32 [2816, 1024], P('heads')
Inputs may be any that keep to these rules, and one draw needn't show every extreme that they name: `segment_ids`: within each aligned block of 512 tokens (one packed row) the ids start at 0 and never fall; each pair holds 256 patches followed by its text, and the padding at a row's end has one id of its own. `padding_mask`: in each packed row the ones form a leading run that ends where the row's last whole pair ends; the rest is 0.
All inputs are finite; a program needn't handle non-finite values.
Results may differ from a plain program's by a relative error of at most 0.024.
Values may be sent and summed in bfloat16 or wider, within the bound.
No kernel may reach another device: no remote copies, remote signals or barrier semaphores. Data moves between devices by JAX's collectives and lax.ppermute only.
A program may use at most 128 MiB of HBM per device.

v0:
```python
import jax
import jax.numpy as jnp
from jax import lax
from jax.sharding import PartitionSpec as P

HEAD_DIM = 64
LEN_MAX = 2048
EPSILON = 1e-06
MASKED = -1000000000.0


def gelu_tanh(values):
    return jax.nn.gelu(values, approximate=True)


def contract(left, right, left_dim, right_dim):
    return lax.dot_general(
        left, right, (((left_dim,), (right_dim,)), ((), ())), preferred_element_type=jnp.float32
    )


def rms_forward(values, gain):
    scale = lax.rsqrt(jnp.mean(values * values, axis=-1, keepdims=True) + EPSILON)
    return (values * scale * gain, scale)


def rms_backward(values, scale, gain, grad_normed):
    unit = values * scale
    grad_unit = grad_normed * gain
    grad_values = scale * (grad_unit - unit * jnp.mean(grad_unit * unit, axis=-1, keepdims=True))
    return (grad_values, jnp.sum(grad_normed * unit, axis=0))


def block_scores(
    queries, key_rows, segments, padding, query_start, row_start, query_count, seq_len
):
    query_block = lax.dynamic_slice_in_dim(queries, query_start, query_count, 0)
    scores = jnp.einsum("qhd,khd->hqk", query_block, key_rows, preferred_element_type=jnp.float32)
    query_segment = lax.dynamic_slice_in_dim(segments, query_start, query_count, 0)
    query_place = query_start + jnp.arange(query_count)
    key_place = row_start + jnp.arange(seq_len)
    allowed = (query_segment[:, None] == segments[None, :]) & (
        (padding[None, :] == 1) | (query_place[:, None] == key_place[None, :])
    )
    return (jnp.where(allowed[None], scores, MASKED), query_block, key_rows)


def attention_forward(queries, key_rows, value_rows, segments, padding, seq_len, query_count):
    group_tokens = queries.shape[0]
    per_seq = seq_len // query_count

    def one_block(number):
        query_start = number * query_count
        row_start = number // per_seq * seq_len
        scores, _, _ = block_scores(
            queries, key_rows, segments, padding, query_start, row_start, query_count, seq_len
        )
        top = jnp.max(scores, axis=-1, keepdims=True)
        expo = jnp.exp(scores - top)
        weight_sum = jnp.sum(expo, axis=-1, keepdims=True)
        probs = (expo / weight_sum).astype(jnp.bfloat16)
        mixed = jnp.einsum("hqk,khd->qhd", probs, value_rows, preferred_element_type=jnp.float32)
        return (mixed.astype(jnp.bfloat16), (top + jnp.log(weight_sum))[:, :, 0])

    mixed, log_sums = lax.map(one_block, jnp.arange(group_tokens // query_count))
    return (mixed.reshape(group_tokens, -1), log_sums)


def attention_backward(
    queries, key_rows, value_rows, segments, padding, log_sums, grad_mixed, seq_len, query_count
):
    group_tokens, heads_here, head_size = queries.shape
    per_seq = seq_len // query_count

    def one_block(carry, item):
        grad_keys, grad_values = carry
        number, log_sum = item
        query_start = number * query_count
        row_start = number // per_seq * seq_len
        scores, query_block, key_block = block_scores(
            queries, key_rows, segments, padding, query_start, row_start, query_count, seq_len
        )
        grad_block = lax.dynamic_slice_in_dim(grad_mixed, query_start, query_count, 0)
        probs = jnp.exp(scores - log_sum[:, :, None])
        grad_probs = jnp.einsum(
            "qhd,khd->hqk", grad_block, value_rows, preferred_element_type=jnp.float32
        )
        grad_scores = probs * (grad_probs - jnp.sum(grad_probs * probs, axis=-1, keepdims=True))
        grad_scores = grad_scores.astype(jnp.bfloat16)
        grad_query = jnp.einsum(
            "hqk,khd->qhd", grad_scores, key_block, preferred_element_type=jnp.float32
        )
        key_part = jnp.einsum(
            "hqk,qhd->khd", grad_scores, query_block, preferred_element_type=jnp.float32
        )
        value_part = jnp.einsum(
            "hqk,qhd->khd",
            probs.astype(jnp.bfloat16),
            grad_block,
            preferred_element_type=jnp.float32,
        )
        grad_keys = grad_keys + key_part
        grad_values = grad_values + value_part
        return ((grad_keys, grad_values), grad_query)

    zero_grads = jnp.zeros((group_tokens, heads_here, head_size), jnp.float32)
    (grad_keys, grad_values), grad_queries = lax.scan(
        one_block, (zero_grads, zero_grads), (jnp.arange(group_tokens // query_count), log_sums)
    )
    return (grad_queries.reshape(group_tokens, heads_here, head_size), grad_keys, grad_values)


def local(
    features,
    segment_ids,
    padding_mask,
    w_proj,
    proj_bias,
    gain_attn,
    w_qkv,
    w_out,
    gain_ffn,
    w_gate_up,
    w_down,
    cotangent,
):
    local_tokens = features.shape[0]
    model_width = w_proj.shape[1]
    attn_cols = w_qkv.shape[2]
    heads_here = attn_cols // HEAD_DIM
    group_tokens = local_tokens * lax.axis_size("heads")
    seq_len = min(LEN_MAX, group_tokens)
    query_count = min(512, seq_len)
    qkv_flat = w_qkv.reshape(model_width, 3 * attn_cols)
    lifted = jnp.dot(features, w_proj, preferred_element_type=jnp.float32) + proj_bias
    normed, scale_attn = rms_forward(lifted, gain_attn)
    gathered, segments, padding = (
        lax.all_gather(normed.astype(jnp.bfloat16), "heads", axis=0, tiled=True),
        lax.all_gather(segment_ids, "heads", axis=0, tiled=True),
        lax.all_gather(padding_mask, "heads", axis=0, tiled=True),
    )
    projected = jnp.dot(gathered, qkv_flat, preferred_element_type=jnp.float32).astype(jnp.bfloat16)
    projected = projected.reshape(group_tokens, 3, heads_here, HEAD_DIM)
    queries, key_rows, value_rows = (projected[:, 0], projected[:, 1], projected[:, 2])
    mixed, log_sums = attention_forward(
        queries, key_rows, value_rows, segments, padding, seq_len, query_count
    )
    middle = lifted + lax.psum_scatter(
        jnp.dot(mixed, w_out, preferred_element_type=jnp.float32).astype(jnp.bfloat16),
        "heads",
        scatter_dimension=0,
        tiled=True,
    ).astype(jnp.float32)
    normed_ffn, scale_ffn = rms_forward(middle, gain_ffn)
    normed_ffn_b = normed_ffn.astype(jnp.bfloat16)
    ff_here = w_gate_up.shape[2]
    gathered_ffn = lax.all_gather(normed_ffn_b, "heads", axis=0, tiled=True)
    gate_flat = w_gate_up.reshape(model_width, 2 * ff_here)
    gate_up = jnp.dot(gathered_ffn, gate_flat, preferred_element_type=jnp.float32)
    activ, gelu_pull = jax.vjp(gelu_tanh, gate_up[:, :ff_here])
    up_part = gate_up[:, ff_here:]
    hidden = (activ * up_part).astype(jnp.bfloat16)
    layer_out = middle + lax.psum_scatter(
        jnp.dot(hidden, w_down, preferred_element_type=jnp.float32).astype(jnp.bfloat16),
        "heads",
        scatter_dimension=0,
        tiled=True,
    ).astype(jnp.float32)
    grad_gathered = lax.all_gather(cotangent, "heads", axis=0, tiled=True)
    grad_hidden = contract(grad_gathered, w_down, 1, 1)
    grad_pre = jnp.concatenate(
        [gelu_pull(grad_hidden * up_part)[0], grad_hidden * activ], axis=1
    ).astype(jnp.bfloat16)
    grad_gu_local = contract(gathered_ffn, grad_pre, 0, 0).reshape(model_width, 2, ff_here)
    grad_down_local = contract(hidden, grad_gathered, 0, 0)
    grad_normed_ffn = lax.psum_scatter(
        contract(grad_pre, gate_flat, 1, 1).astype(jnp.bfloat16),
        "heads",
        scatter_dimension=0,
        tiled=True,
    ).astype(jnp.float32)
    grad_gate_up, grad_down = (
        lax.psum(grad_gu_local.astype(jnp.bfloat16), "rows").astype(jnp.float32),
        lax.psum(grad_down_local.astype(jnp.bfloat16), "rows").astype(jnp.float32),
    )
    grad_ffn_norm, grad_gain_ffn = rms_backward(middle, scale_ffn, gain_ffn, grad_normed_ffn)
    grad_middle = cotangent.astype(jnp.float32) + grad_ffn_norm
    grad_mid_b = grad_middle.astype(jnp.bfloat16)
    grad_attn_in = lax.all_gather(grad_mid_b, "heads", axis=0, tiled=True)
    grad_mixed = contract(grad_attn_in, w_out, 1, 1).astype(jnp.bfloat16)
    grad_out_local = contract(mixed, grad_attn_in, 0, 0)
    grad_queries, grad_keys, grad_values = attention_backward(
        queries,
        key_rows,
        value_rows,
        segments,
        padding,
        log_sums,
        grad_mixed.reshape(group_tokens, heads_here, HEAD_DIM),
        seq_len,
        query_count,
    )
    grad_heads = (
        jnp.stack([grad_queries, grad_keys, grad_values], axis=1)
        .astype(jnp.bfloat16)
        .reshape(group_tokens, 3 * attn_cols)
    )
    grad_qkv_local = contract(gathered, grad_heads, 0, 0).reshape(model_width, 3, attn_cols)
    grad_normed = lax.psum_scatter(
        contract(grad_heads, qkv_flat, 1, 1).astype(jnp.bfloat16),
        "heads",
        scatter_dimension=0,
        tiled=True,
    ).astype(jnp.float32)
    grad_qkv, grad_out = (
        lax.psum(grad_qkv_local.astype(jnp.bfloat16), "rows").astype(jnp.float32),
        lax.psum(grad_out_local.astype(jnp.bfloat16), "rows").astype(jnp.float32),
    )
    grad_attn_norm, grad_gain_attn = rms_backward(lifted, scale_attn, gain_attn, grad_normed)
    grad_lifted = grad_middle + grad_attn_norm
    grad_lift_b = grad_lifted.astype(jnp.bfloat16)
    grad_features = contract(grad_lift_b, w_proj, 1, 1)
    grad_proj_local = contract(features, grad_lift_b, 0, 0)
    grad_proj, grad_bias, grad_gain_attn, grad_gain_ffn = lax.psum(
        (grad_proj_local, jnp.sum(grad_lifted, axis=0), grad_gain_attn, grad_gain_ffn),
        ("rows", "heads"),
    )
    return (
        layer_out.astype(jnp.bfloat16),
        grad_features,
        grad_proj,
        grad_bias,
        grad_gain_attn,
        grad_qkv,
        grad_out,
        grad_gain_ffn,
        grad_gate_up,
        grad_down,
    )


def solution(mesh):
    in_specs = (
        P(("rows", "heads"), None),
        P(("rows", "heads")),
        P(("rows", "heads")),
        P(),
        P(),
        P(),
        P(None, None, "heads"),
        P("heads", None),
        P(),
        P(None, None, "heads"),
        P("heads", None),
        P(("rows", "heads"), None),
    )
    out_specs = (
        P(("rows", "heads"), None),
        P(("rows", "heads"), None),
        P(),
        P(),
        P(),
        P(None, None, "heads"),
        P("heads", None),
        P(),
        P(None, None, "heads"),
        P("heads", None),
    )
    return jax.shard_map(local, mesh=mesh, in_specs=in_specs, out_specs=out_specs, check_vma=False)
```

profile of v0, /device:TPU:0, one launch (start us, length us, event | category | flops | bytes accessed | tf_op | source)
XLA Modules:
  0.0 693.1 jit_solution(15542330360389667371)
XLA Ops:
  13.5 5.1 all-gather.1
  18.7 4.7 copy.39
  23.4 4.3 all-gather
  28.6 9.0 %all-gather.7.cloned.1.call-done = bf16[512,1024]{1,0:T(8,128)(2,1)} async-done(((bf16[256,1024]{1,0:T(8,128)(2,1)}), bf16[512,1024]{1,0:T(8,128)(2,1)}) %all-gather.7.cloned.1.call-update) | async-done | bytes 1048592 | tf_op jit(solution)/shard_map/all_gather | solution.py:138
  37.6 5.2 convolution_convert_fusion.2
  51.5 3.4 fusion.20
  57.5 20.4 %reduce-scatter.5.cloned.1.call-done = bf16[256,1024]{1,0:T(8,128)(2,1)} async-done(((bf16[512,1024]{1,0:T(8,128)(2,1)}), bf16[256,1024]{1,0:T(8,128)(2,1)}) %reduce-scatter.5.cloned.1.call-update) | async-done | bytes 524304 | tf_op jit(solution)/shard_map/reduce_scatter | solution.py:148
  83.0 6.2 copy.53
  89.1 14.2 %all-gather.9.cloned.1.call-done = bf16[512,1024]{1,0:T(8,128)(2,1)} async-done(((bf16[256,1024]{1,0:T(8,128)(2,1)}), bf16[512,1024]{1,0:T(8,128)(2,1)}) %all-gather.9.cloned.1.call-update) | async-done | bytes 1048592 | tf_op jit(solution)/shard_map/all_gather | solution.py:157
  103.3 8.7 %fusion.48 = f32[512,2816]{1,0:T(8,128)} fusion(bf16[512,1024]{1,0:T(8,128)(2,1)} %all-gather.9.cloned.1.call-done, bf16[1024,2816]{1,0:T(8,128)(2,1)} %bitcast.92), kind=kOutput, calls=%fused_computation.90 | convolution fusion | flops 2952790016 | bytes 12582912 | tf_op jit(solution)/shard_map/dot_general | solution.py:159
  112.0 14.2 %all-gather.11.cloned.1.call-done = bf16[512,1024]{1,0:T(8,128)(2,1)} async-done(((bf16[256,1024]{1,0:T(8,128)(2,1)}), bf16[512,1024]{1,0:T(8,128)(2,1)}) %all-gather.11.cloned.1.call-update) | async-done | bytes 1048592 | tf_op jit(solution)/shard_map/all_gather | solution.py:169
  126.1 8.8 %fusion.14 = (bf16[512,1408]{1,0:T(8,128)(2,1)S(1)}, bf16[512,1408]{1,0:T(8,128)(2,1)S(1)}, bf16[512,1408]{1,0:T(8,128)(2,1)}) fusion(f32[512,2816]{1,0:T(8,128)} %fusion.48, bf16[512,1024]{1,0:T(8,128)(2,1)} %all-gather.11.cloned.1.call-done, bf16[1408,1024]{1,0:T(8,128)(2,1)} %param.22), kind=kOutput, calls=%fused_computation.26 | convolution fusion | flops 1495138304 | bytes 14024704 | tf_op jit(solution)/shard_map/dot_general | solution.py:17
  136.5 4.1 fusion.16
  140.7 20.4 %reduce-scatter.9.cloned.1.call-done = bf16[256,1024]{1,0:T(8,128)(2,1)} async-done(((bf16[512,1024]{1,0:T(8,128)(2,1)}), bf16[256,1024]{1,0:T(8,128)(2,1)}) %reduce-scatter.9.cloned.1.call-update) | async-done | bytes 524304 | tf_op jit(solution)/shard_map/reduce_scatter | solution.py:176
  166.3 21.2 %all-gather.13.cloned.1.call-done = bf16[512,1024]{1,0:T(8,128)(2,1)} async-done(((bf16[256,1024]{1,0:T(8,128)(2,1)}), bf16[512,1024]{1,0:T(8,128)(2,1)}) %all-gather.13.cloned.1.call-update) | async-done | bytes 1048592 | tf_op jit(solution)/shard_map/all_gather | solution.py:189
  189.9 5.5 fusion.17
  195.4 5.2 multiply_reduce_fusion
  210.8 5.0 convolution_convert_fusion.5
  215.9 15.3 %reduce-scatter.11.cloned.1.call-done = bf16[256,1024]{1,0:T(8,128)(2,1)} async-done(((bf16[512,1024]{1,0:T(8,128)(2,1)}), bf16[256,1024]{1,0:T(8,128)(2,1)}) %reduce-scatter.11.cloned.1.call-update) | async-done | bytes 524304 | tf_op jit(solution)/shard_map/reduce_scatter | solution.py:209
  233.1 21.4 %reduce-scatter.7.cloned.1.call-done = bf16[256,1024]{1,0:T(8,128)(2,1)} async-done(((bf16[512,1024]{1,0:T(8,128)(2,1)}), bf16[256,1024]{1,0:T(8,128)(2,1)}) %reduce-scatter.7.cloned.1.call-update) | async-done | bytes 524304 | tf_op jit(solution)/shard_map/reduce_scatter | solution.py:163
  254.5 3.6 fusion.46
  258.8 4.0 convolution_bitcast_fusion
  263.2 7.9 %convolution_convert_fusion = bf16[1024,2816]{1,0:T(8,128)(2,1)} fusion(bf16[512,1024]{1,0:T(8,128)(2,1)} %all-gather.9.cloned.1.call-done, bf16[512,1408]{1,0:T(8,128)(2,1)} %copy-done.24, bf16[512,1408]{1,0:T(8,128)(2,1)} %copy-done.23), kind=kOutput, calls=%fused_computation.7 | convolution fusion | flops 2961440768 | bytes 9699328 | tf_op jit(solution)/shard_map/dot_general | solution.py:17
  271.0 12.1 %convert_element_type.141 = bf16[1024,2,1408]{2,1,0:T(2,128)(2,1)} reshape(bf16[1024,2816]{1,0:T(8,128)(2,1)} %convolution_convert_fusion) | data formatting | bytes 11534336 | tf_op jit(solution)/shard_map/convert_element_type | solution.py:183
  283.2 5.1 convolution_convert_fusion.1
  290.2 3.5 convolution_convert_fusion.3
  293.8 40.2 %all-reduce = (f32[1024]{0:T(1024)}, f32[1024]{0:T(1024)}, f32[1024]{0:T(1024)}) all-reduce(f32[1024]{0:T(1024)S(1)} %get-tuple-element.108, f32[1024]{0:T(1024)S(1)} %get-tuple-element.99, f32[1024]{0:T(1024)S(1)} %get-tuple-element.97), channel_id=1, replica_groups=mesh['rows'=16,'heads'=2] {'rows','heads'}, use_global_device_ids=true, to_apply=%region_13.14 | all-reduce | flops 3072 | bytes 24576 | tf_op jit(solution)/shard_map/psum | solution.py:224
  337.4 86.7 %all-reduce.5.cloned.1.call-done = f32[1664,1024]{0,1:T(8,128)} async-done(((f32[1664,1024]{0,1:T(8,128)}), f32[1664,1024]{0,1:T(8,128)}) %all-reduce.5.cloned.1.call-update) | async-done | bytes 6815760 | tf_op jit(solution)/shard_map/psum | solution.py:224
  424.1 7.6 %copy.46 = f32[1664,1024]{1,0:T(8,128)} copy(f32[1664,1024]{0,1:T(8,128)} %all-reduce.5.cloned.1.call-done) | data formatting | bytes 13631488
  431.7 238.1 %all-reduce.7.cloned.1.call-done = (bf16[1024,3,512]{2,0,1:T(8,128)(2,1)}, bf16[512,1024]{1,0:T(8,128)(2,1)}, bf16[1024,2,1408]{2,1,0:T(2,128)(2,1)}, bf16[1408,1024]{1,0:T(8,128)(2,1)}) async-done(((bf16[1024,3,512]{2,0,1:T(8,128)(2,1)}, bf16[512,1024]{1,0:T(8,128)(2,1)}, bf16[1024,2,1408]{2,1,0:T(2,128)(2,1)}, bf16[1408,1024]{1,0:T(8,128)(2,1)}), (bf16[1024,3,512]{2,0,1:T(8,128)(2,1)}, ...) | async-done | bytes 12845072 | tf_op jit(solution)/shard_map/psum | solution.py:216
  669.9 5.6 convert_element_type.137
  677.1 5.7 convert_element_type.142
  (109 shorter events, 55.8 us)
Async XLA Ops:
  7.2 2.0 copy-start
  7.2 5.3 copy-start.15
  7.2 6.3 copy-start.16
  7.2 30.4 %all-gather.7.cloned.1.call-start = ((), (), s32[]{:S(2)}) async-start(), calls=%async_computation.4 | async-start | bytes 1572864 | tf_op jit(solution)/shard_map/all_gather | solution.py:138
  13.5 64.4 %reduce-scatter.5.cloned.1.call-start = ((), (), s32[]{:S(2)}) async-start(), calls=%async_computation.5 | async-start | bytes 1572864 | tf_op jit(solution)/shard_map/reduce_scatter | solution.py:148
  18.7 4.7 copy-start.17
  45.4 2.7 copy-start.4
  48.1 3.4 copy-start.1
  51.5 4.2 copy-start.18
  54.9 24.6 %copy-start.14 = (f32[1024]{0:T(1024)S(1)}, f32[1024]{0:T(1024)}, u32[]{:S(2)}) copy-start(f32[1024]{0:T(1024)} %param.20) | copy-start | bytes 12292
  57.4 45.9 %all-gather.9.cloned.1.call-start = ((), (), s32[]{:S(2)}) async-start(), calls=%async_computation.6 | async-start | bytes 1572864 | tf_op jit(solution)/shard_map/all_gather | solution.py:157
  81.9 44.3 %all-gather.11.cloned.1.call-start = ((), (), s32[]{:S(2)}) async-start(), calls=%async_computation.8 | async-start | bytes 1572864 | tf_op jit(solution)/shard_map/all_gather | solution.py:169
  82.4 78.7 %reduce-scatter.9.cloned.1.call-start = ((), (), s32[]{:S(2)}) async-start(), calls=%async_computation.9 | async-start | bytes 1572864 | tf_op jit(solution)/shard_map/reduce_scatter | solution.py:176
  126.1 10.4 %copy-start.6 = (bf16[128,8,2,1408]{3,1,2,0:T(8,128)(2,1)S(1)}, bf16[128,8,2,1408]{3,1,2,0:T(8,128)(2,1)}, u32[]{:S(2)}) copy-start(bf16[128,8,2,1408]{3,1,2,0:T(8,128)(2,1)} %copy.53) | copy-start | bytes 17301508
  140.7 46.9 %all-gather.13.cloned.1.call-start = ((), (), s32[]{:S(2)}) async-start(), calls=%async_computation.10 | async-start | bytes 1572864 | tf_op jit(solution)/shard_map/all_gather | solution.py:189
  166.1 65.1 %reduce-scatter.11.cloned.1.call-start = ((), (), s32[]{:S(2)}) async-start(), calls=%async_computation.11 | async-start | bytes 1572864 | tf_op jit(solution)/shard_map/reduce_scatter | solution.py:209
  187.5 2.3 copy-start.5
  189.9 5.5 copy-start.3
  189.9 10.7 %slice-start = ((s8[8388608]{0:T(1024)(128)(4,1)}), s8[4194304]{0:T(1024)(128)(4,1)S(1)}, s32[]{:S(2)}) async-start(s8[8388608]{0:T(1024)(128)(4,1)} %bitcast.82), calls=%async_computation.14 | async-start | bytes 8388608
  195.4 5.2 slice-start.1
  205.5 2.5 copy-start.7
  210.7 43.7 %reduce-scatter.7.cloned.1.call-start = ((), (), s32[]{:S(2)}) async-start(), calls=%async_computation.7 | async-start | bytes 1572864 | tf_op jit(solution)/shard_map/reduce_scatter | solution.py:163
  215.8 208.3 %all-reduce.5.cloned.1.call-start = ((), (), s32[]{:S(2)}) async-start(), calls=%async_computation.12 | async-start | bytes 13631488 | tf_op jit(solution)/shard_map/psum | solution.py:224
  254.5 4.4 copy-start.13
  262.9 406.9 %all-reduce.7.cloned.1.call-start = ((), (), s32[]{:S(2)}) async-start(), calls=%async_computation.13 | async-start | bytes 25690112 | tf_op jit(solution)/shard_map/psum | solution.py:216
  283.1 5.1 copy-start.20
  283.1 5.1 copy-start.22
  288.3 1.9 copy-start.19
  669.9 7.2 %slice-start.2 = ((s8[5767168]{0:T(1024)(128)(4,1)}), s8[4194304]{0:T(1024)(128)(4,1)S(1)}, s32[]{:S(2)}) async-start(s8[5767168]{0:T(1024)(128)(4,1)} %bitcast.90), calls=%async_computation.16 | async-start | bytes 8388608
  669.9 5.7 copy-start.12
  669.9 7.2 %slice-start.3 = ((s8[5767168]{0:T(1024)(128)(4,1)}), s8[1572864]{0:T(1024)(128)(4,1)S(1)}, s32[]{:S(2)}) async-start(s8[5767168]{0:T(1024)(128)(4,1)} %bitcast.90), calls=%async_computation.17 | async-start | bytes 3145728
  677.1 5.8 copy-start.8
  (7 other events, 8.2 us)
Sparse Core Ops, SparseCore 0:
  13.6 23.9 all-gather.6
  57.6 20.3 reduce-scatter.4
  82.0 21.3 all-gather.8
  104.8 21.2 all-gather.10
  140.8 20.3 reduce-scatter.8
  166.2 21.2 all-gather.12
  210.9 20.3 reduce-scatter.10
  234.1 20.3 reduce-scatter.6
  263.0 161.0 all-reduce.4
  429.7 240.1 all-reduce.6
where the time goes:
time: 701 us; the launch traced here: 693 us
  waiting for transfers between devices  462 us (66%)
  matrix products  85.5 us (12%)
  blocking collectives  49.6 us (7%)
  local copies, waits for them, and re-layouts  43.6 us (6%)
  other arithmetic  36.7 us (5%)
  between operations  14.7 us (2%)
    psum x1, waiting for transfers between devices, local(): lax.psum(grad_qkv_local.astype(jnp.bfloat16), 'rows').astype(jnp.float32)  238 us
    psum x1, waiting for transfers between devices, local(): lax.psum((grad_proj_local, jnp.sum(grad_lifted, axis=0), grad_gain_attn,...  86.7 us
    dot_general x10, matrix products, contract(): lax.dot_general(left, right, (((left_dim,), (right_dim,)), ((), ())), pre...  43.7 us
    psum x1, blocking collectives, local(): lax.psum((grad_proj_local, jnp.sum(grad_lifted, axis=0), grad_gain_attn,...  40.2 us
    unnamed x61, local copies, waits for them, and re-layouts  28.9 us
    reduce_scatter x1, waiting for transfers between devices, local(): lax.psum_scatter(jnp.dot(hidden, w_down, preferred_element_type=jnp.float...  21.4 us
    all_gather x1, waiting for transfers between devices, local(): grad_attn_in = lax.all_gather(grad_mid_b, 'heads', axis=0, tiled=True)  21.2 us
    reduce_scatter x1, waiting for transfers between devices, local(): lax.psum_scatter(jnp.dot(mixed, w_out, preferred_element_type=jnp.float32...  20.4 us
  transfers between devices with their start and end apart: 10, of which 10 were waited for; matrix products, arithmetic and copies ran while one was open for 10% of the time, Pallas kernels for 0%

commit v1 on v0

--- a/solution.py
+++ b/solution.py
@@ -213,7 +213,9 @@
         tiled=True,
     ).astype(jnp.float32)
     grad_qkv, grad_out = (
-        lax.psum(grad_qkv_local.astype(jnp.bfloat16), "rows").astype(jnp.float32),
+        jnp.sum(lax.all_gather(grad_qkv_local.astype(jnp.bfloat16), "rows"), axis=0).astype(
+            jnp.float32
+        ),
         lax.psum(grad_out_local.astype(jnp.bfloat16), "rows").astype(jnp.float32),
     )
     grad_attn_norm, grad_gain_attn = rms_backward(lifted, scale_attn, gain_attn, grad_normed)

time: 701 us -> 905 us (1.29)
  waiting for transfers between devices: 462 us -> 643 us
  other arithmetic: 36.7 us -> 56.2 us
    all_gather x0 -> x1, waiting for transfers between devices: none -> 241 us  [local(): lax.all_gather(grad_qkv_local.astype(jnp.bfloat16), 'rows')]
    psum x1, waiting for transfers between devices: 238 us -> 137 us  [local(): lax.psum(grad_out_local.astype(jnp.bfloat16), 'rows').astype(jnp.float32)]
    psum x1, waiting for transfers between devices: 86.7 us -> 155 us  [local(): lax.psum((grad_proj_local, jnp.sum(grad_lifted, axis=0), grad_gain_attn,...]
    reduce_sum x0 -> x1, other arithmetic: none -> 18.3 us  [local(): jnp.sum(lax.all_gather(grad_qkv_local.astype(jnp.bfloat16), 'rows'), axis=0)]
    reduce_scatter x1, waiting for transfers between devices: 15.3 us -> 0.02 us  [local(): lax.psum_scatter(contract(grad_heads, qkv_flat, 1, 1).astype(jnp.bfloat16...]
    reduce_scatter x1, waiting for transfers between devices: 21.4 us -> 9.5 us  [local(): lax.psum_scatter(jnp.dot(hidden, w_down, preferred_element_type=jnp.float...]
    unnamed x61 -> x55, local copies, waits for them, and re-layouts: 28.9 us -> 28.7 us
  transfers between devices with their start and end apart: 10 -> 11, of which waited for: 10 -> 10; matrix products, arithmetic and copies ran while one was open for 10% -> 10% of each run, Pallas kernels for 0% -> 0%
where the time goes in v1:
time: 905 us; the launch traced here: 897 us
  waiting for transfers between devices  643 us (71%)
  matrix products  87.4 us (10%)
  other arithmetic  56.2 us (6%)
  blocking collectives  51.4 us (6%)
  local copies, waits for them, and re-layouts  43.4 us (5%)
  between operations  14.4 us (2%)
    all_gather x1, waiting for transfers between devices, local(): lax.all_gather(grad_qkv_local.astype(jnp.bfloat16), 'rows')  241 us
    psum x1, waiting for transfers between devices, local(): lax.psum((grad_proj_local, jnp.sum(grad_lifted, axis=0), grad_gain_attn,...  155 us
    psum x1, waiting for transfers between devices, local(): lax.psum(grad_out_local.astype(jnp.bfloat16), 'rows').astype(jnp.float32)  137 us
    dot_general x10, matrix products, contract(): lax.dot_general(left, right, (((left_dim,), (right_dim,)), ((), ())), pre...  45.5 us
    psum x1, blocking collectives, local(): lax.psum((grad_proj_local, jnp.sum(grad_lifted, axis=0), grad_gain_attn,...  42 us
    unnamed x55, local copies, waits for them, and re-layouts  28.7 us
    all_gather x1, waiting for transfers between devices, local(): grad_attn_in = lax.all_gather(grad_mid_b, 'heads', axis=0, tiled=True)  21.2 us
    reduce_scatter x1, waiting for transfers between devices, local(): lax.psum_scatter(jnp.dot(mixed, w_out, preferred_element_type=jnp.float32...  20.4 us
  transfers between devices with their start and end apart: 11, of which 10 were waited for; matrix products, arithmetic and copies ran while one was open for 10% of the time, Pallas kernels for 0%

profile of v1, /device:TPU:0, one launch (start us, length us, event | category | flops | bytes accessed | tf_op | source)
XLA Modules:
  0.0 897.5 jit_solution(9307884641021011760)
XLA Ops:
  13.5 5.1 all-gather.2
  18.7 4.7 copy.39
  23.4 4.3 all-gather.1
  28.6 9.0 %all-gather.9.cloned.1.call-done = bf16[512,1024]{1,0:T(8,128)(2,1)} async-done(((bf16[256,1024]{1,0:T(8,128)(2,1)}), bf16[512,1024]{1,0:T(8,128)(2,1)}) %all-gather.9.cloned.1.call-update) | async-done | bytes 1048592 | tf_op jit(solution)/shard_map/all_gather | solution.py:138
  37.6 5.2 convolution_convert_fusion.2
  57.5 20.4 %reduce-scatter.5.cloned.1.call-done = bf16[256,1024]{1,0:T(8,128)(2,1)} async-done(((bf16[512,1024]{1,0:T(8,128)(2,1)}), bf16[256,1024]{1,0:T(8,128)(2,1)}) %reduce-scatter.5.cloned.1.call-update) | async-done | bytes 524304 | tf_op jit(solution)/shard_map/reduce_scatter | solution.py:148
  83.0 6.2 copy.53
  89.2 14.1 %all-gather.11.cloned.1.call-done = bf16[512,1024]{1,0:T(8,128)(2,1)} async-done(((bf16[256,1024]{1,0:T(8,128)(2,1)}), bf16[512,1024]{1,0:T(8,128)(2,1)}) %all-gather.11.cloned.1.call-update) | async-done | bytes 1048592 | tf_op jit(solution)/shard_map/all_gather | solution.py:157
  103.4 8.7 fusion.48
  112.0 14.2 %all-gather.13.cloned.1.call-done = bf16[512,1024]{1,0:T(8,128)(2,1)} async-done(((bf16[256,1024]{1,0:T(8,128)(2,1)}), bf16[512,1024]{1,0:T(8,128)(2,1)}) %all-gather.13.cloned.1.call-update) | async-done | bytes 1048592 | tf_op jit(solution)/shard_map/all_gather | solution.py:169
  126.2 8.8 fusion.14
  136.5 4.1 fusion.16
  140.7 20.4 %reduce-scatter.9.cloned.1.call-done = bf16[256,1024]{1,0:T(8,128)(2,1)} async-done(((bf16[512,1024]{1,0:T(8,128)(2,1)}), bf16[256,1024]{1,0:T(8,128)(2,1)}) %reduce-scatter.9.cloned.1.call-update) | async-done | bytes 524304 | tf_op jit(solution)/shard_map/reduce_scatter | solution.py:176
  166.3 21.2 %all-gather.15.cloned.1.call-done = bf16[512,1024]{1,0:T(8,128)(2,1)} async-done(((bf16[256,1024]{1,0:T(8,128)(2,1)}), bf16[512,1024]{1,0:T(8,128)(2,1)}) %all-gather.15.cloned.1.call-update) | async-done | bytes 1048592 | tf_op jit(solution)/shard_map/all_gather | solution.py:189
  189.9 5.5 fusion.17
  195.4 5.2 multiply_reduce_fusion
  210.8 5.0 convolution_convert_fusion.5
  216.1 8.1 convolution_convert_fusion
  224.2 12.1 %convert_element_type.143 = bf16[1024,2,1408]{2,1,0:T(2,128)(2,1)} reshape(bf16[1024,2816]{1,0:T(8,128)(2,1)} %convolution_convert_fusion) | data formatting | bytes 11534336 | tf_op jit(solution)/shard_map/convert_element_type | solution.py:183
  236.3 5.0 convolution_convert_fusion.1
  244.9 9.5 %reduce-scatter.7.cloned.1.call-done = bf16[256,1024]{1,0:T(8,128)(2,1)} async-done(((bf16[512,1024]{1,0:T(8,128)(2,1)}), bf16[256,1024]{1,0:T(8,128)(2,1)}) %reduce-scatter.7.cloned.1.call-update) | async-done | bytes 524304 | tf_op jit(solution)/shard_map/reduce_scatter | solution.py:163
  254.5 3.6 fusion.46
  258.8 4.0 convolution_bitcast_fusion
  263.0 5.2 convolution_convert_fusion.3
  268.2 42.0 %all-reduce = (f32[1024]{0:T(1024)}, f32[1024]{0:T(1024)}, f32[1024]{0:T(1024)}) all-reduce(f32[1024]{0:T(1024)S(1)} %get-tuple-element.107, f32[1024]{0:T(1024)S(1)} %get-tuple-element.99, f32[1024]{0:T(1024)S(1)} %get-tuple-element.97), channel_id=1, replica_groups=mesh['rows'=16,'heads'=2] {'rows','heads'}, use_global_device_ids=true, to_apply=%region_13.14 | all-reduce | flops 3072 | bytes 24576 | tf_op jit(solution)/shard_map/psum | solution.py:226
  313.5 137.3 %all-reduce.7.cloned.1.call-done = (bf16[512,1024]{1,0:T(8,128)(2,1)}, bf16[1024,2,1408]{2,1,0:T(2,128)(2,1)}, bf16[1408,1024]{1,0:T(8,128)(2,1)}) async-done(((bf16[512,1024]{1,0:T(8,128)(2,1)}, bf16[1024,2,1408]{2,1,0:T(2,128)(2,1)}, bf16[1408,1024]{1,0:T(8,128)(2,1)}), (bf16[512,1024]{1,0:T(8,128)(2,1)}, bf16[1024,2,1408]{2,1,0:T(2,128)(2,1)}, bf16[1408,1024]{1,0:T(8,128)(2,1)})) %all-reduce.7.cloned.1.call-update) | async-done | bytes 9699344 | tf_op jit(solution)/shard_map/psum | solution.py:219
  457.0 5.7 convert_element_type.144
  462.8 155.4 %all-reduce.5.cloned.1.call-done = f32[1664,1024]{0,1:T(8,128)} async-done(((f32[1664,1024]{0,1:T(8,128)}), f32[1664,1024]{0,1:T(8,128)}) %all-reduce.5.cloned.1.call-update) | async-done | bytes 6815760 | tf_op jit(solution)/shard_map/psum | solution.py:226
  618.2 7.6 copy.46
  625.8 241.1 %all-gather.17.cloned.1.call-done = bf16[16384,3,512]{2,0,1:T(8,128)(2,1)} async-done(((bf16[1024,3,512]{2,0,1:T(8,128)(2,1)}), bf16[16384,3,512]{2,0,1:T(8,128)(2,1)}) %all-gather.17.cloned.1.call-update) | async-done | bytes 50331664 | tf_op jit(solution)/shard_map/all_gather | solution.py:216
  866.9 18.3 %reduce_sum.103 = bf16[1024,3,512]{2,0,1:T(8,128)(2,1)} reduce(bf16[16,1024,3,512]{3,1,0,2:T(8,128)(2,1)} %bitcast.85, bf16[]{:T(256)} %constant.91.clone.1), dimensions={0}, to_apply=%region_16.17 | reduce | flops 23592960 | bytes 53477376 | tf_op jit(solution)/shard_map/reduce_sum | solution.py:216
  885.2 5.5 convert_element_type.139
  (107 shorter events, 60.5 us)
Async XLA Ops:
  7.2 2.0 copy-start
  7.2 5.3 copy-start.13
  7.2 6.3 copy-start.14
  7.2 30.4 %all-gather.9.cloned.1.call-start = ((), (), s32[]{:S(2)}) async-start(), calls=%async_computation.4 | async-start | bytes 1572864 | tf_op jit(solution)/shard_map/all_gather | solution.py:138
  13.5 64.5 %reduce-scatter.5.cloned.1.call-start = ((), (), s32[]{:S(2)}) async-start(), calls=%async_computation.5 | async-start | bytes 1572864 | tf_op jit(solution)/shard_map/reduce_scatter | solution.py:148
  18.7 4.7 copy-start.15
  45.4 2.7 copy-start.4
  48.1 3.4 copy-start.1
  51.5 4.2 copy-start.16
  55.0 24.6 %copy-start.12 = (f32[1024]{0:T(1024)S(1)}, f32[1024]{0:T(1024)}, u32[]{:S(2)}) copy-start(f32[1024]{0:T(1024)} %param.20) | copy-start | bytes 12292
  57.5 45.9 %all-gather.11.cloned.1.call-start = ((), (), s32[]{:S(2)}) async-start(), calls=%async_computation.6 | async-start | bytes 1572864 | tf_op jit(solution)/shard_map/all_gather | solution.py:157
  81.9 44.3 %all-gather.13.cloned.1.call-start = ((), (), s32[]{:S(2)}) async-start(), calls=%async_computation.8 | async-start | bytes 1572864 | tf_op jit(solution)/shard_map/all_gather | solution.py:169
  82.5 78.7 %reduce-scatter.9.cloned.1.call-start = ((), (), s32[]{:S(2)}) async-start(), calls=%async_computation.9 | async-start | bytes 1572864 | tf_op jit(solution)/shard_map/reduce_scatter | solution.py:176
  126.2 10.4 %copy-start.6 = (bf16[128,8,2,1408]{3,1,2,0:T(8,128)(2,1)S(1)}, bf16[128,8,2,1408]{3,1,2,0:T(8,128)(2,1)}, u32[]{:S(2)}) copy-start(bf16[128,8,2,1408]{3,1,2,0:T(8,128)(2,1)} %copy.53) | copy-start | bytes 17301508
  135.0 1.6 copy-start.21
  140.7 46.8 %all-gather.15.cloned.1.call-start = ((), (), s32[]{:S(2)}) async-start(), calls=%async_computation.10 | async-start | bytes 1572864 | tf_op jit(solution)/shard_map/all_gather | solution.py:189
  166.1 77.0 %reduce-scatter.11.cloned.1.call-start = ((), (), s32[]{:S(2)}) async-start(), calls=%async_computation.11 | async-start | bytes 1572864 | tf_op jit(solution)/shard_map/reduce_scatter | solution.py:209
  187.5 2.3 copy-start.5
  189.9 5.5 copy-start.3
  189.9 10.7 %slice-start = ((s8[8388608]{0:T(1024)(128)(4,1)}), s8[4194304]{0:T(1024)(128)(4,1)S(1)}, s32[]{:S(2)}) async-start(s8[8388608]{0:T(1024)(128)(4,1)} %bitcast.83), calls=%async_computation.15 | async-start | bytes 8388608
  195.4 5.2 slice-start.1
  205.5 2.5 copy-start.7
  210.7 43.7 %reduce-scatter.7.cloned.1.call-start = ((), (), s32[]{:S(2)}) async-start(), calls=%async_computation.7 | async-start | bytes 1572864 | tf_op jit(solution)/shard_map/reduce_scatter | solution.py:163
  215.8 235.0 %all-reduce.7.cloned.1.call-start = ((), (), s32[]{:S(2)}) async-start(), calls=%async_computation.14 | async-start | bytes 19398656 | tf_op jit(solution)/shard_map/psum | solution.py:219
  236.3 5.0 copy-start.17
  236.3 5.1 copy-start.19
  243.0 375.1 %all-reduce.5.cloned.1.call-start = ((), (), s32[]{:S(2)}) async-start(), calls=%async_computation.12 | async-start | bytes 13631488 | tf_op jit(solution)/shard_map/psum | solution.py:226
  254.5 4.4 copy-start.11
  262.9 604.0 %all-gather.17.cloned.1.call-start = ((), (), s32[]{:S(2)}) async-start(), calls=%async_computation.13 | async-start | bytes 53477376 | tf_op jit(solution)/shard_map/all_gather | solution.py:216
  450.8 2.9 copy-start.8
  450.8 6.2 slice-start.2
  453.8 3.3 slice-start.3
  (5 other events, 4.8 us)
Sparse Core Ops, SparseCore 0:
  13.6 23.9 all-gather.8
  57.6 20.3 reduce-scatter.4
  82.0 21.3 all-gather.10
  104.8 21.2 all-gather.12
  140.8 20.3 reduce-scatter.8
  166.2 21.2 all-gather.14
  210.8 20.3 reduce-scatter.10
  234.1 20.3 reduce-scatter.6
  259.6 191.1 all-reduce.6
  457.0 161.1 all-reduce.4
  619.7 247.1 all-gather.16
